TPU v7x, 512 devices: a whole 4x4x16 slice. The times are simulated.
512 devices in a mesh: batch: 64 (over z, y), proto: 8 (over x, core).
Axes of the slice: x: 4, y: 4, z: 16, core: 2. Of those that a mesh axis runs over, the one named last changes fastest.
Arguments:
- embeddings: bfloat16 [65536, 256], P('batch'), as said below
- prototypes: bfloat16 [16384, 256], P('proto'), as said below
- partner: int32 [65536], P('batch'), may hold values from 0 to 65535, as said below
Outputs:
- emb_grad: float32 [65536, 256], P('batch')
- proto_grad: float32 [16384, 256], P('proto')
Inputs may be any that keep to these rules, and one draw needn't show every extreme that they name: partner[partner[b]] == b for every view b, and partner[b] lies in the aligned block of 1024 views whose block index differs from that of b by 32. `embeddings`: no row is zero. `prototypes`: no row is zero.
All inputs are finite; a program needn't handle non-finite values.
Results may differ from a plain program's by a relative error of at most 0.0016.
Values may be sent and summed in bfloat16 or wider, within the bound.
No kernel may reach another device: no remote copies, remote signals or barrier semaphores. Data moves between devices by JAX's collectives and lax.ppermute only.
A program may use at most 64 MiB of HBM per device.

v0:
```python
import jax
import jax.numpy as jnp
from jax import lax
from jax.sharding import PartitionSpec as P

ITERS = 3
epsilon_code = 0.05
sharpness_divisor = 0.1
norm_floor = 1e-06


def shifted(value, axis, steps):
    count = lax.axis_size(axis)
    pairs = [(source, (source + steps) % count) for source in range(count)]
    return lax.ppermute(value, axis, pairs)


def unit_rows(values):
    wide = values.astype(jnp.float32)
    scale = lax.rsqrt(jnp.mean(wide * wide, axis=1, keepdims=True) + norm_floor) / jnp.sqrt(
        jnp.float32(wide.shape[1])
    )
    return (wide * scale, scale)


def norm_back(upstream, units, scale):
    return scale * (upstream - units * jnp.sum(units * upstream, axis=1, keepdims=True))


def contract_rows(left, right):
    return lax.dot_general(
        left, right, (((0,), (0,)), ((), ())), preferred_element_type=jnp.float32
    )


def body(embeddings, prototypes, partner):
    view_units, view_scale = unit_rows(embeddings)
    proto_units, proto_scale = unit_rows(prototypes)
    views = view_units.astype(jnp.bfloat16)
    protos = proto_units.astype(jnp.bfloat16)
    row_count = views.shape[0]
    links = jnp.remainder(partner, row_count)
    separation_measure = lax.axis_size("batch") // 2
    centroid_raw_affinities = jnp.dot(views, protos.T, preferred_element_type=jnp.float32)
    kernel = jnp.exp(centroid_raw_affinities / epsilon_code)

    def column_scale_of(weight):
        column_part = jnp.sum(weight[:, None] * kernel, axis=0)
        return 1.0 / lax.psum(column_part, "batch")

    weight = jnp.ones((row_count,), jnp.float32)
    for sweep in range(ITERS - 1):
        column_scale = column_scale_of(weight)
        row_part = jnp.sum(kernel * column_scale[None, :], axis=1)
        weight = 1.0 / lax.psum(row_part, "proto")
    column_scale = column_scale_of(weight)
    tempered_affinities = jnp.exp(centroid_raw_affinities / sharpness_divisor)
    soft_part = jnp.sum(tempered_affinities, axis=1)
    dispersion_width = kernel * column_scale[None, :]
    line_aggregate, soft_total = lax.psum((jnp.sum(dispersion_width, axis=1), soft_part), "proto")
    balanced_transport_labels = (dispersion_width * (1.0 / line_aggregate)[:, None]).astype(
        jnp.bfloat16
    )
    received_pieces = shifted(balanced_transport_labels, "batch", separation_measure)
    centroid_agreement = received_pieces[links]
    estimated_likelihood = tempered_affinities * (1.0 / soft_total)[:, None]
    logit_gradient = (
        (estimated_likelihood - centroid_agreement.astype(jnp.float32)) / sharpness_divisor
    ).astype(jnp.bfloat16)
    view_part = jnp.dot(logit_gradient, protos, preferred_element_type=jnp.float32)
    view_upstream = lax.psum(view_part, "proto")
    emb_grad = norm_back(view_upstream, view_units, view_scale)
    proto_upstream = lax.psum(contract_rows(logit_gradient, views), "batch")
    proto_grad = norm_back(proto_upstream, proto_units, proto_scale)
    return (emb_grad, proto_grad)


def solution(mesh):
    return jax.shard_map(
        body,
        mesh=mesh,
        in_specs=(P("batch", None), P("proto", None), P("batch")),
        out_specs=(P("batch", None), P("proto", None)),
        check_vma=False,
    )
```

profile of v0, /device:TPU:2, one launch (start us, length us, event | category | flops | bytes accessed | tf_op | source)
XLA Modules:
  0.0 1267.4 jit_solution(6247067676049251214)
XLA Ops:
  10.1 6.3 fusion.4
  16.3 151.9 %psum.64 = f32[2048]{0:T(1024)S(1)} all-reduce(f32[2048]{0:T(1024)S(1)} %get-tuple-element.6), channel_id=1, replica_groups=mesh['batch'=64,'proto'=8] {'batch'}, use_global_device_ids=true, to_apply=%region_5.6 | all-reduce | flops 2048 | bytes 16384 | tf_op jit(solution)/shard_map/psum | solution.py:49
  168.3 5.1 fusion
  173.4 10.0 psum.65
  183.4 4.3 multiply_reduce_fusion.2
  187.7 140.0 %psum.66 = f32[2048]{0:T(1024)S(1)} all-reduce(f32[2048]{0:T(1024)S(1)} %multiply_reduce_fusion.2), channel_id=1, replica_groups=mesh['batch'=64,'proto'=8] {'batch'}, use_global_device_ids=true, to_apply=%region_9.10 | all-reduce | flops 2048 | bytes 16384 | tf_op jit(solution)/shard_map/psum | solution.py:49
  327.8 4.8 multiply_reduce_fusion.1
  332.6 11.9 psum.67
  344.5 4.3 multiply_reduce_fusion
  348.8 142.1 %psum.68 = f32[2048]{0:T(1024)S(1)} all-reduce(f32[2048]{0:T(1024)S(1)} %multiply_reduce_fusion), channel_id=1, replica_groups=mesh['batch'=64,'proto'=8] {'batch'}, use_global_device_ids=true, to_apply=%region_13.14 | all-reduce | flops 2048 | bytes 16384 | tf_op jit(solution)/shard_map/psum | solution.py:49
  490.9 4.8 multiply_reduce_fusion.4
  495.8 12.6 all-reduce
  508.4 4.4 multiply_convert_fusion.1
  512.8 6.5 collective-permute-start
  519.4 293.3 %collective-permute-done = bf16[1024,2048]{1,0:T(8,128)(2,1)} collective-permute-done((bf16[1024,2048]{1,0:T(8,128)(2,1)S(1)}, bf16[1024,2048]{1,0:T(8,128)(2,1)}, u32[]{:S(2)}, u32[]{:S(2)}) %collective-permute-start) | collective-permute-done | bytes 4194336 | tf_op jit(solution)/shard_map/ppermute | solution.py:15
  812.7 11.6 gather_fusion
  824.2 6.1 multiply_convert_fusion
  832.2 2.3 fusion.16
  834.7 5.0 fusion.20
  839.7 131.9 %all-reduce.4.cloned.1.call-done = f32[1024,256]{1,0:T(8,128)} async-done(((f32[1024,256]{1,0:T(8,128)}), f32[1024,256]{1,0:T(8,128)}) %all-reduce.4.cloned.1.call-update) | async-done | bytes 1048592 | tf_op jit(solution)/shard_map/psum | solution.py:71
  973.2 2.5 fusion.14
  975.7 279.7 %all-reduce.6.cloned.1.call-done = f32[2048,256]{1,0:T(8,128)} async-done(((f32[2048,256]{1,0:T(8,128)}), f32[2048,256]{1,0:T(8,128)}) %all-reduce.6.cloned.1.call-update) | async-done | bytes 2097168 | tf_op jit(solution)/shard_map/psum | solution.py:73
  1255.4 2.2 fusion.5
  1257.7 2.9 fusion.7
  (25 shorter events, 6.5 us)
Async XLA Ops:
  7.2 964.4 %all-reduce.4.cloned.1.call-start = ((), (), s32[]{:S(2)}) async-start(), calls=%async_computation | async-start | bytes 2097152 | tf_op jit(solution)/shard_map/psum | solution.py:71
  495.8 23.6 %copy-start.3 = (s32[1024]{0:T(1024)S(1)}, s32[1024]{0:T(1024)}, u32[]{:S(2)}) copy-start(s32[1024]{0:T(1024)} %param.5) | copy-start | bytes 12292
  512.8 299.9 %collective-permute-start = (bf16[1024,2048]{1,0:T(8,128)(2,1)S(1)}, bf16[1024,2048]{1,0:T(8,128)(2,1)}, u32[]{:S(2)}, u32[]{:S(2)}) collective-permute-start(bf16[1024,2048]{1,0:T(8,128)(2,1)S(1)} %multiply_convert_fusion.1), channel_id=1, source_target_pairs={{0,256},{8,264},{16,272},{24,280},{32,288},{40,296},{48,304},{56,3... | collective-permute-start | bytes 12582920 | tf_op jit(solution)/shard_map/ppermute | solution.py:15
  824.2 8.0 copy-start
  830.3 1.9 copy-start.2
  832.2 2.4 copy-start.1
  834.6 420.9 %all-reduce.6.cloned.1.call-start = ((), (), s32[]{:S(2)}) async-start(), calls=%async_computation.1 | async-start | bytes 4194304 | tf_op jit(solution)/shard_map/psum | solution.py:73
Sparse Core Ops, SparseCore 0:
  834.7 136.8 all-reduce.3
  975.6 279.7 all-reduce.5
where the time goes:
time: 1270 us
  waiting for transfers between devices  705 us (56%)
  blocking collectives  469 us (37%)
  other arithmetic  45.9 us (4%)
  between operations  14.2 us (1%)
  matrix products  13.6 us (1%)
  local copies, waits for them, and re-layouts  13.5 us (1%)
    psum x3, blocking collectives, column_scale_of(): return 1.0 / lax.psum(column_part, 'batch')  434 us
    ppermute x1, waiting for transfers between devices, shifted(): return lax.ppermute(value, axis, pairs)  293 us
    psum x1, waiting for transfers between devices, body(): proto_upstream = lax.psum(contract_rows(logit_gradient, views), 'batch')  280 us
    psum x1, waiting for transfers between devices, body(): view_upstream = lax.psum(view_part, 'proto')  132 us
  transfers between devices with their start and end apart: 3, of which 3 were waited for; matrix products, arithmetic and copies ran while one was open for 1% of the time, Pallas kernels for 0%

commit v1 on v0

--- a/solution.py
+++ b/solution.py
@@ -68,7 +68,11 @@
         (estimated_likelihood - centroid_agreement.astype(jnp.float32)) / sharpness_divisor
     ).astype(jnp.bfloat16)
     view_part = jnp.dot(logit_gradient, protos, preferred_element_type=jnp.float32)
-    view_upstream = lax.psum(view_part, "proto")
+    view_upstream = view_part
+    for hop in (1, 2, 4):
+        view_upstream = view_upstream + lax.ppermute(
+            view_upstream, "proto", [(dev, dev ^ hop) for dev in range(8)]
+        )
     emb_grad = norm_back(view_upstream, view_units, view_scale)
     proto_upstream = lax.psum(contract_rows(logit_gradient, views), "batch")
     proto_grad = norm_back(proto_upstream, proto_units, proto_scale)

time: 1270 us -> 1190 us (0.937)
  waiting for transfers between devices: 705 us -> 624 us
    psum x1 -> x0, waiting for transfers between devices: 132 us -> none  [body(): view_upstream = lax.psum(view_part, 'proto')]
    psum x1, waiting for transfers between devices: 280 us -> 307 us  [body(): proto_upstream = lax.psum(contract_rows(logit_gradient, views), 'batch')]
    ppermute x0 -> x3, waiting for transfers between devices: none -> 23.8 us  [body(): lax.ppermute(view_upstream, 'proto', [(dev, dev ^ hop) for dev in range(8)])]
  transfers between devices with their start and end apart: 3 -> 5, of which waited for: 3 -> 3; matrix products, arithmetic and copies ran while one was open for 1% -> 1% of each run, Pallas kernels for 0% -> 0%
where the time goes in v1:
time: 1190 us
  waiting for transfers between devices  624 us (52%)
  blocking collectives  469 us (39%)
  other arithmetic  43.9 us (4%)
  starting transfers between devices  16.4 us (1%)
  between operations  14.3 us (1%)
  local copies, waits for them, and re-layouts  14.1 us (1%)
    psum x3, blocking collectives, column_scale_of(): return 1.0 / lax.psum(column_part, 'batch')  434 us
    psum x1, waiting for transfers between devices, body(): proto_upstream = lax.psum(contract_rows(logit_gradient, views), 'batch')  307 us
    ppermute x1, waiting for transfers between devices, shifted(): return lax.ppermute(value, axis, pairs)  293 us
    ppermute x3, waiting for transfers between devices, body(): lax.ppermute(view_upstream, 'proto', [(dev, dev ^ hop) for dev in range(8)])  23.8 us
  transfers between devices with their start and end apart: 5, of which 3 were waited for; matrix products, arithmetic and copies ran while one was open for 1% of the time, Pallas kernels for 0%

profile of v1, /device:TPU:2, one launch (start us, length us, event | category | flops | bytes accessed | tf_op | source)
XLA Modules:
  0.0 1191.7 jit_solution(12283345561146257793)
XLA Ops:
  10.2 6.4 fusion.4
  16.6 151.9 %psum.57 = f32[2048]{0:T(1024)S(1)} all-reduce(f32[2048]{0:T(1024)S(1)} %get-tuple-element.10), channel_id=1, replica_groups=mesh['batch'=64,'proto'=8] {'batch'}, use_global_device_ids=true, to_apply=%region_5.6 | all-reduce | flops 2048 | bytes 16384 | tf_op jit(solution)/shard_map/psum | solution.py:49
  168.5 5.1 fusion
  173.6 10.0 psum.58
  183.7 4.3 multiply_reduce_fusion.2
  188.0 140.0 %psum.59 = f32[2048]{0:T(1024)S(1)} all-reduce(f32[2048]{0:T(1024)S(1)} %multiply_reduce_fusion.2), channel_id=1, replica_groups=mesh['batch'=64,'proto'=8] {'batch'}, use_global_device_ids=true, to_apply=%region_9.10 | all-reduce | flops 2048 | bytes 16384 | tf_op jit(solution)/shard_map/psum | solution.py:49
  328.0 4.8 multiply_reduce_fusion.1
  332.8 11.9 psum.60
  344.7 4.3 multiply_reduce_fusion
  349.0 142.1 %psum.61 = f32[2048]{0:T(1024)S(1)} all-reduce(f32[2048]{0:T(1024)S(1)} %multiply_reduce_fusion), channel_id=1, replica_groups=mesh['batch'=64,'proto'=8] {'batch'}, use_global_device_ids=true, to_apply=%region_13.14 | all-reduce | flops 2048 | bytes 16384 | tf_op jit(solution)/shard_map/psum | solution.py:49
  491.2 4.8 multiply_reduce_fusion.4
  496.0 12.6 %all-reduce = (f32[1024]{0:T(1024)S(1)}, f32[1024]{0:T(1024)S(1)}) all-reduce(f32[1024]{0:T(1024)S(1)} %multiply_reduce_fusion.4, f32[1024]{0:T(1024)S(1)} %get-tuple-element.4), channel_id=1, replica_groups=mesh['batch'=64,'proto'=8] {'proto'}, use_global_device_ids=true, to_apply=%region_15.16 | all-reduce | flops 2048 | bytes 16384 | tf_op jit(solution)/shard_map/psum | solution.py:60
  508.7 4.4 multiply_convert_fusion.1
  513.0 6.5 collective-permute-start
  519.6 293.0 %collective-permute-done = bf16[1024,2048]{1,0:T(8,128)(2,1)} collective-permute-done((bf16[1024,2048]{1,0:T(8,128)(2,1)S(1)}, bf16[1024,2048]{1,0:T(8,128)(2,1)}, u32[]{:S(2)}, u32[]{:S(2)}) %collective-permute-start) | collective-permute-done | bytes 4194336 | tf_op jit(solution)/shard_map/ppermute | solution.py:15
  812.6 11.6 gather_fusion
  824.2 6.1 multiply_convert_fusion
  833.6 2.7 fusion.16
  837.7 5.4 collective-permute-start.2
  843.2 23.8 %collective-permute-done.2 = f32[1024,256]{0,1:T(8,128)S(1)} collective-permute-done((f32[1024,256]{0,1:T(8,128)S(1)}, f32[1024,256]{0,1:T(8,128)S(1)}, u32[]{:S(2)}, u32[]{:S(2)}) %collective-permute-start.2) | collective-permute-done | bytes 1048608 | tf_op jit(solution)/shard_map/ppermute | solution.py:73
  867.1 2.5 collective-permute-start.3
  869.6 307.1 %all-reduce.3.cloned.1.call-done = f32[2048,256]{1,0:T(8,128)} async-done(((f32[2048,256]{1,0:T(8,128)}), f32[2048,256]{1,0:T(8,128)}) %all-reduce.3.cloned.1.call-update) | async-done | bytes 2097168 | tf_op jit(solution)/shard_map/psum | solution.py:77
  1176.7 2.2 fusion.5
  1179.0 2.9 fusion.7
  (28 shorter events, 11.0 us)
Async XLA Ops:
  7.2 1169.6 %all-reduce.3.cloned.1.call-start = ((), (), s32[]{:S(2)}) async-start(), calls=%async_computation | async-start | bytes 4194304 | tf_op jit(solution)/shard_map/psum | solution.py:77
  496.0 23.6 %copy-start.1 = (s32[1024]{0:T(1024)S(1)}, s32[1024]{0:T(1024)}, u32[]{:S(2)}) copy-start(s32[1024]{0:T(1024)} %param.5) | copy-start | bytes 12292
  513.0 299.6 %collective-permute-start = (bf16[1024,2048]{1,0:T(8,128)(2,1)S(1)}, bf16[1024,2048]{1,0:T(8,128)(2,1)}, u32[]{:S(2)}, u32[]{:S(2)}) collective-permute-start(bf16[1024,2048]{1,0:T(8,128)(2,1)S(1)} %multiply_convert_fusion.1), channel_id=1, source_target_pairs={{0,256},{8,264},{16,272},{24,280},{32,288},{40,296},{48,304},{56,3... | collective-permute-start | bytes 12582920 | tf_op jit(solution)/shard_map/ppermute | solution.py:15
  824.2 6.1 copy-start
  831.7 4.7 collective-permute-start.1
  837.7 29.2 %collective-permute-start.2 = (f32[1024,256]{0,1:T(8,128)S(1)}, f32[1024,256]{0,1:T(8,128)S(1)}, u32[]{:S(2)}, u32[]{:S(2)}) collective-permute-start(f32[1024,256]{0,1:T(8,128)S(1)} %add.63), channel_id=1, source_target_pairs={{0,2},{1,3},{2,0},{3,1},{4,6},{5,7},{6,4},{7,5},{8,10},{9,11},{10,... | collective-permute-start | bytes 3145736 | tf_op jit(solution)/shard_map/ppermute | solution.py:73
  867.1 314.7 %collective-permute-start.3 = (f32[1024,256]{0,1:T(8,128)S(1)}, f32[1024,256]{0,1:T(8,128)}, u32[]{:S(2)}, u32[]{:S(2)}) collective-permute-start(f32[1024,256]{0,1:T(8,128)S(1)} %add.64), channel_id=1, source_target_pairs={{0,4},{1,5},{2,6},{3,7},{4,0},{5,1},{6,2},{7,3},{8,12},{9,13},{10,... | collective-permute-start | bytes 3145736 | tf_op jit(solution)/shard_map/ppermute | solution.py:73
Sparse Core Ops, SparseCore 0:
  836.5 340.2 all-reduce.2
